TPU v7x, 32 devices: a whole 2x2x4 slice. The times are simulated.
32 devices in a mesh: section: 2 (over core), dp: 8 (over z, x), rep: 2 (over y).
Axes of the slice: x: 2, y: 2, z: 4, core: 2. Of those that a mesh axis runs over, the one named last changes fastest.
Arguments:
- inputs: bfloat16 [4096, 1024], P(('dp', 'rep')), may hold values from -6 to 6
- cotangent: bfloat16 [4096, 1024], P(('dp', 'rep')), may hold values from -6 to 6
- seg_counts: int32 [256], P(('dp', 'rep')), may hold values from 2 to 16
- w_qkv: bfloat16 [2, 1024, 3072], P('section'), may hold values from -0.1875 to 0.1875
- w_out: bfloat16 [2, 1024, 1024], P('section'), may hold values from -0.375 to 0.375
- w_up: bfloat16 [2, 1024, 2048], P('section'), may hold values from -0.1875 to 0.1875
- w_down: bfloat16 [2, 2048, 1024], P('section'), may hold values from -0.1875 to 0.1875
- gains: float32 [2, 2, 1024], P('section'), may hold values from 0.5 to 1.5
- biases: float32 [2, 2, 1024], P('section'), may hold values from -3 to 3
Outputs:
- layer_outputs: bfloat16 [2, 4096, 1024], P('section', ('dp', 'rep'))
- input_grads: bfloat16 [2, 4096, 1024], P('section', ('dp', 'rep'))
- grad_qkv: float32 [2, 1024, 3072], P('section', 'dp')
- grad_wout: float32 [2, 1024, 1024], P('section', None, 'dp')
- grad_up: float32 [2, 1024, 2048], P('section', 'dp')
- grad_down: float32 [2, 2048, 1024], P('section', None, 'dp')
- grad_gains: float32 [2, 2, 1024], P('section', None, 'dp')
- grad_biases: float32 [2, 2, 1024], P('section', None, 'dp')
Inputs may be any that keep to these rules, and one draw needn't show every extreme that they name: seg_counts gives each series' number of valid slots; the first 16 - seg_counts slots of a series are padding.
All inputs are finite; a program needn't handle non-finite values.
Results may differ from a plain program's by a relative error of at most 0.015.
Values may be sent and summed in bfloat16 or wider, within the bound.
A program may use at most 256 MiB of HBM per device.

v0:
```python
from functools import partial
import jax
import jax.numpy as jnp
from jax import lax
from jax.sharding import PartitionSpec as P

SEG = 16
HEAD_DIM = 128
BLOCK = 128
epsilon = 1e-05
f32 = jnp.float32
bf16 = jnp.bfloat16


def normalize(hidden):
    average = jnp.mean(hidden, axis=-1, keepdims=True)
    centred = hidden - average
    inverse = lax.rsqrt(jnp.mean(centred * centred, axis=-1, keepdims=True) + epsilon)
    return (centred * inverse, inverse)


def normalize_back(grad_normed, normed, inverse):
    centre_term = jnp.mean(grad_normed, axis=-1, keepdims=True)
    slope_term = normed * jnp.mean(grad_normed * normed, axis=-1, keepdims=True)
    return inverse * (grad_normed - centre_term - slope_term)


def allowed_pairs(counts):
    rows = counts.shape[0] * SEG
    blocks = rows // BLOCK
    ids = jnp.arange(rows, dtype=jnp.int32).reshape(blocks, BLOCK)
    first = jnp.repeat(SEG - counts, SEG).reshape(blocks, BLOCK)
    position = ids % SEG
    owner = ids // SEG
    same = owner[:, :, None] == owner[:, None, :]
    causal = position[:, None, :] <= position[:, :, None]
    valid = (position >= first)[:, None, :] | (ids[:, :, None] == ids[:, None, :])
    return same & causal & valid


def forward(hidden_b, params, allowed):
    w_qkv, w_out, w_up, w_down, gains, biases = params
    rows = hidden_b.shape[0]
    heads = w_qkv.shape[1] // (3 * HEAD_DIM)
    hidden = hidden_b.astype(f32)
    n1, i1 = normalize(hidden)
    a = (n1 * gains[0] + biases[0]).astype(bf16)
    packed = jnp.dot(a, w_qkv, preferred_element_type=f32).astype(bf16)
    split = packed.reshape(rows // BLOCK, BLOCK, 3, heads, HEAD_DIM)
    scores = jnp.einsum(
        "bqhd,bkhd->bhqk", split[:, :, 0], split[:, :, 1], preferred_element_type=f32
    )
    scores = jnp.where(allowed[:, None], scores * HEAD_DIM ** (-0.5), -1e30)
    raised = jnp.exp(scores - jnp.max(scores, axis=-1, keepdims=True))
    probs = raised / jnp.sum(raised, axis=-1, keepdims=True)
    probs_b = probs.astype(bf16)
    mixed = jnp.einsum("bhqk,bkhd->bqhd", probs_b, split[:, :, 2], preferred_element_type=f32)
    mixed_b = mixed.reshape(rows, heads * HEAD_DIM).astype(bf16)
    middle = hidden + jnp.dot(mixed_b, w_out, preferred_element_type=f32)
    n2, i2 = normalize(middle)
    c = (n2 * gains[1] + biases[1]).astype(bf16)
    upper = jnp.dot(c, w_up, preferred_element_type=f32)
    g = jax.nn.gelu(upper, approximate=True).astype(bf16)
    result = (middle + jnp.dot(g, w_down, preferred_element_type=f32)).astype(bf16)
    return (result, (n1, i1, a, split, probs, probs_b, mixed_b, n2, i2, c, upper, g))


def backward(saved, grad_b, params):
    w_qkv, w_out, w_up, w_down, gains, biases = params
    n1, i1, a, split, probs, probs_b, mixed_b, n2, i2, c, upper, g = saved
    rows = grad_b.shape[0]
    heads = w_qkv.shape[1] // (3 * HEAD_DIM)
    d_g = jnp.einsum("rd,fd->rf", grad_b, w_down, preferred_element_type=f32)
    d_u = jax.vjp(partial(jax.nn.gelu, approximate=True), upper)[1](d_g)[0].astype(bf16)
    d_c = jnp.einsum("rf,df->rd", d_u, w_up, preferred_element_type=f32)
    d_m = grad_b.astype(f32) + normalize_back(d_c * gains[1], n2, i2)
    d_mb = d_m.astype(bf16)
    d_o = jnp.einsum("ro,io->ri", d_mb, w_out, preferred_element_type=f32).astype(bf16)
    d_o = d_o.reshape(rows // BLOCK, BLOCK, heads, HEAD_DIM)
    d_probs = jnp.einsum("bqhd,bkhd->bhqk", d_o, split[:, :, 2], preferred_element_type=f32)
    d_v = jnp.einsum("bhqk,bqhd->bkhd", probs_b, d_o, preferred_element_type=f32)
    d_s = (probs * (d_probs - jnp.sum(probs * d_probs, axis=-1, keepdims=True))).astype(bf16)
    d_q = jnp.einsum(
        "bhqk,bkhd->bqhd", d_s, split[:, :, 1], preferred_element_type=f32
    ) * HEAD_DIM ** (-0.5)
    d_k = jnp.einsum(
        "bhqk,bqhd->bkhd", d_s, split[:, :, 0], preferred_element_type=f32
    ) * HEAD_DIM ** (-0.5)
    d_p = jnp.stack((d_q, d_k, d_v), axis=2).reshape(rows, -1).astype(bf16)
    d_a = jnp.einsum("re,de->rd", d_p, w_qkv, preferred_element_type=f32)
    d_h = (d_m + normalize_back(d_a * gains[0], n1, i1)).astype(bf16)
    return (d_h, (d_u, d_mb, d_p, d_a, d_c))


def per_device(inputs, cotangent, seg_counts, w_qkv, w_out, w_up, w_down, gains, biases):
    last = lax.axis_size("section") - 1
    section = lax.axis_index("section")
    params = (w_qkv[0], w_out[0], w_up[0], w_down[0], gains[0], biases[0])
    allowed = allowed_pairs(seg_counts)
    sent = forward(inputs, params, allowed)[0]
    hidden = jnp.where(section == 0, inputs, lax.ppermute(sent, "section", [(0, 1)]))
    result, saved = forward(hidden, params, allowed)
    sent = backward(saved, cotangent, params)[0]
    grad = jnp.where(section == last, cotangent, lax.ppermute(sent, "section", [(1, 0)]))
    d_h, (d_u, d_mb, d_p, d_a, d_c) = backward(saved, grad, params)
    n1, i1, a, split, probs, probs_b, mixed_b, n2, i2, c, upper, g = saved

    def outer(left, right):
        return jnp.einsum("ri,ro->io", left, right, preferred_element_type=f32).astype(bf16)[None]

    terms = (outer(a, d_p), outer(mixed_b, d_mb), outer(c, d_u), outer(g, grad))
    small_g = jnp.stack((jnp.sum(d_a * n1, axis=0), jnp.sum(d_c * n2, axis=0)))[None]
    small_b = jnp.stack((jnp.sum(d_a, axis=0), jnp.sum(d_c, axis=0)))[None]
    terms = terms + (small_g, small_b)
    dims = (1, 2, 1, 2, 2, 2)
    shares = [
        lax.psum_scatter(term, "dp", scatter_dimension=dim, tiled=True)
        for term, dim in zip(terms, dims)
    ]
    summed = [lax.psum(share.astype(bf16), "rep").astype(f32) for share in shares]
    return (result[None], d_h[None], *summed)


def solution(mesh):
    rows = P(("dp", "rep"), None)
    layer = P("section", None, None)
    return jax.shard_map(
        per_device,
        mesh=mesh,
        in_specs=(rows, rows, P(("dp", "rep"))) + (layer,) * 6,
        out_specs=(
            P("section", ("dp", "rep"), None),
            P("section", ("dp", "rep"), None),
            P("section", "dp", None),
            P("section", None, "dp"),
            P("section", "dp", None),
            P("section", None, "dp"),
            P("section", None, "dp"),
            P("section", None, "dp"),
        ),
        check_vma=False,
    )
```

profile of v0, /device:TPU:0, one launch (start us, length us, event | category | flops | bytes accessed | tf_op | source)
XLA Modules:
  0.0 717.0 jit_solution(17454511011516978575)
XLA Ops:
  12.4 4.9 fusion.63
  26.4 7.5 %fusion.93 = bf16[256,1024]{1,0:T(8,128)(2,1)} fusion(f32[256,1024]{1,0:T(8,128)} %copy-done.15, bf16[1,2048,1024]{2,1,0:T(8,128)(2,1)} %param.15, bf16[1,1024,2048]{2,1,0:T(8,128)(2,1)} %param.14, f32[1024]{0:T(1024)S(1)} %bitcast.290, f32[1024]{0:T(1024)S(1)} %bitcast.281, f32[256]{0:T(256)S(1)} %add_rsqrt_fusion.2, f32[256]{0:T(256)S(1)} %broadcast_multiply_fusion.10), kind=kOutput, calls=%fused_computation.92 | convolution fusion | flops 2154037248 | bytes 9971712 | tf_op jit(solution)/shard_map/dot_general | solution.py:64
  38.5 4.7 fusion.60
  58.3 8.4 %fusion.198 = (f32[256]{0:T(256)S(1)}, f32[256]{0:T(256)S(1)}, f32[256,1024]{1,0:T(8,128)}) fusion(f32[256]{0:T(256)S(1)} %add_rsqrt_fusion, f32[256,1024]{1,0:T(8,128)S(1)} %get-tuple-element.43, f32[256]{0:T(256)S(1)} %broadcast_multiply_fusion.8, f32[1024]{0:T(1024)S(1)} %bitcast.283, bf16[1,1024,2048]{2,1,0:T(8,128)(2,1)} %param.14, ...), kind=kOutput, calls=%fused_computation.231 | convolution fusion | flops 2159541760 | bytes 13115392 | tf_op jit(solution)/shard_map/rf,df->rd/dot_general | solution.py:75
  79.1 11.6 %pad_maximum_fusion = bf16[2,128,3,8,128]{4,1,3,0,2:T(8,128)(2,1)S(1)} fusion(bf16[2,128,1,8,128]{4,1,3,0,2:T(8,128)(2,1)S(1)} %copy-done.25, bf16[2,128,1,8,128]{4,1,3,0,2:T(8,128)(2,1)S(1)} %fusion.114, bf16[2,128,1,8,128]{4,1,3,0,2:T(8,128)(2,1)S(1)} %fusion.115), kind=kLoop, calls=%fused_computation.63 | loop fusion | flops 1572864 | bytes 3145728 | tf_op jit(solution)/shard_map/stack | solution.py:89
  92.8 3.7 convert_element_type.182
  96.6 5.4 fusion.197
  108.8 5.4 add_convert_fusion
  119.6 10.8 %copy.135 = bf16[1,1024,1024]{1,0,2:T(2,128)(2,1)} copy(bf16[1,1024,1024]{2,1,0:T(8,128)(2,1)} %convert_bitcast_fusion.3) | data formatting | bytes 4194304
  130.5 4.3 copy.188
  134.8 5.3 convert_bitcast_fusion.1
  140.1 20.6 %copy.137 = bf16[1,2048,1024]{1,0,2:T(2,128)(2,1)} copy(bf16[1,2048,1024]{2,1,0:T(8,128)(2,1)} %convert_bitcast_fusion.1) | data formatting | bytes 8388608
  160.7 8.0 %copy.187 = bf16[1024,1,2048]{2,0,1:T(8,128)(2,1)} copy(bf16[1024,1,2048]{2,1,0:T(2,128)(2,1)} %bitcast.260) | data formatting | bytes 8388608
  168.8 5.0 convert_bitcast_fusion.2
  191.1 6.2 convert_bitcast_fusion
  197.4 6.4 fusion.140
  209.9 85.5 %reduce-scatter.21.cloned.1.call-done = bf16[128,2048]{1,0:T(8,128)(2,1)} async-done(((bf16[1024,2048]{1,0:T(8,128)(2,1)}), bf16[128,2048]{1,0:T(8,128)(2,1)}) %reduce-scatter.21.cloned.1.call-update) | async-done | bytes 524304
  301.6 85.6 %reduce-scatter.17.cloned.1.call-done = bf16[1,128,2048]{2,1,0:T(8,128)(2,1)} async-done(((bf16[1,1024,2048]{2,1,0:T(8,128)(2,1)}), bf16[1,128,2048]{2,1,0:T(8,128)(2,1)}) %reduce-scatter.17.cloned.1.call-update) | async-done | bytes 524304 | tf_op jit(solution)/shard_map/reduce_scatter | solution.py:117
  387.2 121.2 %reduce-scatter.15.cloned.1.call-done = bf16[1,128,3072]{2,1,0:T(8,128)(2,1)} async-done(((bf16[1,1024,3072]{2,1,0:T(8,128)(2,1)}), bf16[1,128,3072]{2,1,0:T(8,128)(2,1)}) %reduce-scatter.15.cloned.1.call-update) | async-done | bytes 786448 | tf_op jit(solution)/shard_map/reduce_scatter | solution.py:117
  508.5 5.5 fusion.122
  515.2 57.5 %reduce-scatter.25.cloned.1.call-done = f32[128,2]{1,0:T(8,128)} async-done(((f32[1024,2]{1,0:T(8,128)}), f32[128,2]{1,0:T(8,128)}) %reduce-scatter.25.cloned.1.call-update) | async-done | bytes 1040
  573.6 64.2 %reduce-scatter.23.cloned.1.call-done = f32[128,2]{1,0:T(8,128)} async-done(((f32[1024,2]{1,0:T(8,128)}), f32[128,2]{1,0:T(8,128)}) %reduce-scatter.23.cloned.1.call-update) | async-done | bytes 1040
  638.7 4.9 all-reduce
  644.7 58.6 %all-reduce.4.cloned.1.call-done = (bf16[1,128,3072]{2,1,0:T(8,128)(2,1)}, bf16[1,1024,128]{2,1,0:T(8,128)(2,1)}, bf16[1,128,2048]{2,1,0:T(8,128)(2,1)}, bf16[1,2048,128]{2,1,0:T(8,128)(2,1)}) async-done(((bf16[1,128,3072]{2,1,0:T(8,128)(2,1)}, bf16[1,1024,128]{2,1,0:T(8,128)(2,1)}, bf16[1,128,2048]{2,1,0:T(8,128)(2,1)}, bf16[1,2048,128]{2,1,0:T(8,128)(2,1)}), (bf16[1,128,3072]{2,1,0:T(8,128)(2,1)}, ...) | async-done | bytes 2097168 | tf_op jit(solution)/shard_map/psum | solution.py:120
  (168 shorter events, 100.6 us)
Async XLA Ops:
  7.2 17.2 %copy-start = (bf16[1,1024,1024]{2,1,0:T(8,128)(2,1)S(1)}, bf16[1,1024,1024]{2,1,0:T(8,128)(2,1)}, u32[]{:S(2)}) copy-start(bf16[1,1024,1024]{2,1,0:T(8,128)(2,1)} %param.13) | copy-start | bytes 6291460
  7.2 198.8 %reduce-scatter.19.cloned.1.call-start = ((), (), s32[]{:S(2)}) async-start(), calls=%async_computation.8 | async-start | bytes 2359296
  20.2 4.2 copy-start.7
  33.9 4.1 collective-permute-start
  38.2 5.1 copy-start.2
  44.7 5.1 copy-start.9
  44.7 5.1 copy-start.12
  55.2 59.0 %copy-start.1 = (f32[256,1024]{1,0:T(8,128)}, f32[256,1024]{1,0:T(8,128)S(1)}, u32[]{:S(2)}) copy-start(f32[256,1024]{1,0:T(8,128)S(1)} %get-tuple-element.43) | copy-start | bytes 3145732
  96.6 5.5 copy-start.3
  96.6 5.5 copy-start.16
  96.6 5.5 copy-start.21
  103.5 4.1 collective-permute-start.1
  108.8 7.1 copy-start.17
  108.8 5.4 copy-start.27
  134.8 160.7 %reduce-scatter.21.cloned.1.call-start = ((), (), s32[]{:S(2)}) async-start(), calls=%async_computation.9 | async-start | bytes 4718592
  168.8 218.4 %reduce-scatter.17.cloned.1.call-start = ((), (), s32[]{:S(2)}) async-start(), calls=%async_computation.7 | async-start | bytes 4718592 | tf_op jit(solution)/shard_map/reduce_scatter | solution.py:117
  173.8 334.6 %reduce-scatter.15.cloned.1.call-start = ((), (), s32[]{:S(2)}) async-start(), calls=%async_computation.6 | async-start | bytes 7077888 | tf_op jit(solution)/shard_map/reduce_scatter | solution.py:117
  197.3 375.4 %reduce-scatter.25.cloned.1.call-start = ((), (), s32[]{:S(2)}) async-start(), calls=%async_computation.11 | async-start | bytes 589824
  204.8 432.9 %reduce-scatter.23.cloned.1.call-start = ((), (), s32[]{:S(2)}) async-start(), calls=%async_computation.10 | async-start | bytes 589824
  206.0 497.3 %all-reduce.4.cloned.1.call-start = ((), (), s32[]{:S(2)}) async-start(), calls=%async_computation.12 | async-start | bytes 4194304 | tf_op jit(solution)/shard_map/psum | solution.py:120
  508.4 5.5 copy-start.4
  508.4 5.5 copy-start.18
  703.3 4.3 copy-start.23
  705.1 3.6 copy-start.22
  (14 other events, 19.8 us)
Sparse Core Ops, SparseCore 0:
  134.9 69.7 reduce-scatter.18
  208.3 87.0 reduce-scatter.20
  299.5 87.6 reduce-scatter.16
  390.6 117.7 reduce-scatter.14
  511.6 61.0 reduce-scatter.24
  576.8 60.8 reduce-scatter.22
  640.8 62.4 all-reduce.3
where the time goes:
time: 725 us; the launch traced here: 717 us
  waiting for transfers between devices  477 us (66%)
  matrix products  94.3 us (13%)
  local copies, waits for them, and re-layouts  90 us (12%)
  other arithmetic  31.2 us (4%)
  between operations  15.1 us (2%)
    unnamed x11, waiting for transfers between devices  207 us
    reduce_scatter x2, waiting for transfers between devices, per_device(): lax.psum_scatter(term, 'dp', scatter_dimension=dim, tiled=True)  207 us
    unnamed x76, local copies, waits for them, and re-layouts  68.5 us
    psum x1, waiting for transfers between devices, per_device(): lax.psum(share.astype(bf16), 'rep').astype(f32)  58.6 us
    dot_general x4, matrix products, outer(): jnp.einsum('ri,ro->io', left, right, preferred_element_type=f32)  18.5 us
  transfers between devices with their start and end apart: 9, of which 8 were waited for; matrix products, arithmetic and copies ran while one was open for 12% of the time, Pallas kernels for 0%

commit v1 on v0

--- a/solution.py
+++ b/solution.py
@@ -117,7 +117,9 @@
         lax.psum_scatter(term, "dp", scatter_dimension=dim, tiled=True)
         for term, dim in zip(terms, dims)
     ]
-    summed = [lax.psum(share.astype(bf16), "rep").astype(f32) for share in shares]
+    summed = [
+        jnp.sum(lax.all_gather(share.astype(bf16), "rep"), axis=0).astype(f32) for share in shares
+    ]
     return (result[None], d_h[None], *summed)
 
 

time: 725 us -> 702 us (0.968)
  waiting for transfers between devices: 477 us -> 451 us
  blocking collectives: 4.94 us -> 15.5 us
  other arithmetic: 31.2 us -> 22.9 us
    reduce_scatter x2, waiting for transfers between devices: 207 us -> 111 us  [per_device(): lax.psum_scatter(term, 'dp', scatter_dimension=dim, tiled=True)]
    unnamed x11 -> x13, waiting for transfers between devices: 207 us -> 277 us
    all_gather x0 -> x3, waiting for transfers between devices: none -> 59.1 us  [per_device(): lax.all_gather(share.astype(bf16), 'rep')]
    psum x1 -> x0, waiting for transfers between devices: 58.6 us -> none  [per_device(): lax.psum(share.astype(bf16), 'rep').astype(f32)]
    all_gather x0 -> x3, blocking collectives: none -> 15.5 us  [per_device(): lax.all_gather(share.astype(bf16), 'rep')]
    another operation x1, other arithmetic: 11.6 us -> 0.38 us  [backward(): d_p = jnp.stack((d_q, d_k, d_v), axis=2).reshape(rows, -1).astype(bf16)]
    unnamed x76 -> x70, local copies, waits for them, and re-layouts: 68.5 us -> 67.5 us
  transfers between devices with their start and end apart: 9 -> 11, of which waited for: 8 -> 10; matrix products, arithmetic and copies ran while one was open for 12% -> 16% of each run, Pallas kernels for 0% -> 0%
where the time goes in v1:
time: 702 us; the launch traced here: 694 us
  waiting for transfers between devices  451 us (64%)
  matrix products  96.1 us (14%)
  local copies, waits for them, and re-layouts  89.1 us (13%)
  other arithmetic  22.9 us (3%)
  blocking collectives  15.5 us (2%)
  between operations  14.6 us (2%)
    unnamed x13, waiting for transfers between devices  277 us
    reduce_scatter x2, waiting for transfers between devices, per_device(): lax.psum_scatter(term, 'dp', scatter_dimension=dim, tiled=True)  111 us
    unnamed x70, local copies, waits for them, and re-layouts  67.5 us
    all_gather x3, waiting for transfers between devices, per_device(): lax.all_gather(share.astype(bf16), 'rep')  59.1 us
    dot_general x4, matrix products, outer(): jnp.einsum('ri,ro->io', left, right, preferred_element_type=f32)  18 us
    all_gather x3, blocking collectives, per_device(): lax.all_gather(share.astype(bf16), 'rep')  15.5 us
  transfers between devices with their start and end apart: 11, of which 10 were waited for; matrix products, arithmetic and copies ran while one was open for 16% of the time, Pallas kernels for 0%

profile of v1, /device:TPU:0, one launch (start us, length us, event | category | flops | bytes accessed | tf_op | source)
XLA Modules:
  0.0 693.7 jit_solution(1856469828723809944)
XLA Ops:
  12.4 4.9 fusion.63
  26.4 7.5 %fusion.93 = bf16[256,1024]{1,0:T(8,128)(2,1)} fusion(f32[256,1024]{1,0:T(8,128)} %copy-done.14, bf16[1,2048,1024]{2,1,0:T(8,128)(2,1)} %param.15, bf16[1,1024,2048]{2,1,0:T(8,128)(2,1)} %param.14, f32[1024]{0:T(1024)S(1)} %bitcast.308, f32[1024]{0:T(1024)S(1)} %bitcast.299, f32[256]{0:T(256)S(1)} %add_rsqrt_fusion.2, f32[256]{0:T(256)S(1)} %broadcast_multiply_fusion.10), kind=kOutput, calls=%fused_computation.92 | convolution fusion | flops 2154037248 | bytes 9971712 | tf_op jit(solution)/shard_map/dot_general | solution.py:64
  38.5 4.7 fusion.60
  58.2 8.4 %fusion.198 = (f32[256]{0:T(256)S(1)}, f32[256]{0:T(256)S(1)}, f32[256,1024]{1,0:T(8,128)}) fusion(f32[256]{0:T(256)S(1)} %add_rsqrt_fusion, f32[256,1024]{1,0:T(8,128)S(1)} %get-tuple-element.37, f32[256]{0:T(256)S(1)} %broadcast_multiply_fusion.8, f32[1024]{0:T(1024)S(1)} %bitcast.301, bf16[1,1024,2048]{2,1,0:T(8,128)(2,1)} %param.14, ...), kind=kOutput, calls=%fused_computation.237 | convolution fusion | flops 2159541760 | bytes 13115392 | tf_op jit(solution)/shard_map/rf,df->rd/dot_general | solution.py:75
  85.3 5.4 fusion.197
  97.5 5.3 add_convert_fusion
  107.3 5.3 convert_bitcast_fusion.1
  112.5 20.6 %copy.137 = bf16[1,2048,1024]{1,0,2:T(2,128)(2,1)} copy(bf16[1,2048,1024]{2,1,0:T(8,128)(2,1)} %convert_bitcast_fusion.1) | data formatting | bytes 8388608
  133.2 8.2 %copy.187 = bf16[1024,1,2048]{2,0,1:T(8,128)(2,1)} copy(bf16[1024,1,2048]{2,1,0:T(2,128)(2,1)} %bitcast.278) | data formatting | bytes 8388608
  164.7 6.3 fusion.140
  173.2 6.2 convert_bitcast_fusion
  182.9 10.9 %copy.135 = bf16[1,1024,1024]{1,0,2:T(2,128)(2,1)} copy(bf16[1,1024,1024]{2,1,0:T(8,128)(2,1)} %convert_bitcast_fusion.3) | data formatting | bytes 4194304
  193.8 4.4 copy.188
  199.0 90.5 %reduce-scatter.21.cloned.1.call-done = bf16[128,2048]{1,0:T(8,128)(2,1)} async-done(((bf16[1024,2048]{1,0:T(8,128)(2,1)}), bf16[128,2048]{1,0:T(8,128)(2,1)}) %reduce-scatter.21.cloned.1.call-update) | async-done | bytes 524304
  295.7 5.5 fusion.122
  302.4 52.1 %reduce-scatter.25.cloned.1.call-done = f32[128,2]{1,0:T(8,128)} async-done(((f32[1024,2]{1,0:T(8,128)}), f32[128,2]{1,0:T(8,128)}) %reduce-scatter.25.cloned.1.call-update) | async-done | bytes 1040
  355.4 63.5 %reduce-scatter.23.cloned.1.call-done = f32[128,2]{1,0:T(8,128)} async-done(((f32[1024,2]{1,0:T(8,128)}), f32[128,2]{1,0:T(8,128)}) %reduce-scatter.23.cloned.1.call-update) | async-done | bytes 1040
  419.8 4.2 all-gather.5
  428.8 110.6 %reduce-scatter.15.cloned.1.call-done = bf16[1,128,3072]{2,1,0:T(8,128)(2,1)} async-done(((bf16[1,1024,3072]{2,1,0:T(8,128)(2,1)}), bf16[1,128,3072]{2,1,0:T(8,128)(2,1)}) %reduce-scatter.15.cloned.1.call-update) | async-done | bytes 786448 | tf_op jit(solution)/shard_map/reduce_scatter | solution.py:117
  540.0 69.8 %reduce-scatter.19.cloned.1.call-done = bf16[128,1024]{1,0:T(8,128)(2,1)} async-done(((bf16[1024,1024]{1,0:T(8,128)(2,1)}), bf16[128,1024]{1,0:T(8,128)(2,1)}) %reduce-scatter.19.cloned.1.call-update) | async-done | bytes 262160
  611.5 7.0 %all-gather.1 = bf16[2,1024,128]{2,1,0:T(8,128)(2,1)S(1)} all-gather(bf16[1,1024,128]{2,1,0:T(8,128)(2,1)S(1)} %copy.136), channel_id=3, replica_groups=mesh['section'=2,'dp'=8,'rep'=2] {'rep'}, dimensions={0}, use_global_device_ids=true | all-gather | bytes 786432 | tf_op jit(solution)/shard_map/all_gather | solution.py:121
  619.6 12.1 %all-gather.12.cloned.1.call-done = bf16[2,128,2048]{2,1,0:T(8,128)(2,1)} async-done(((bf16[1,128,2048]{2,1,0:T(8,128)(2,1)}), bf16[2,128,2048]{2,1,0:T(8,128)(2,1)}) %all-gather.12.cloned.1.call-update) | async-done | bytes 1048592 | tf_op jit(solution)/shard_map/all_gather | solution.py:121
  633.1 22.0 %all-gather.14.cloned.1.call-done = bf16[2,2048,128]{2,1,0:T(8,128)(2,1)} async-done(((bf16[1,2048,128]{2,1,0:T(8,128)(2,1)}), bf16[2,2048,128]{2,1,0:T(8,128)(2,1)}) %all-gather.14.cloned.1.call-update) | async-done | bytes 1048592 | tf_op jit(solution)/shard_map/all_gather | solution.py:121
  659.0 25.0 %all-gather.10.cloned.1.call-done = bf16[2,128,3072]{2,1,0:T(8,128)(2,1)} async-done(((bf16[1,128,3072]{2,1,0:T(8,128)(2,1)}), bf16[2,128,3072]{2,1,0:T(8,128)(2,1)}) %all-gather.10.cloned.1.call-update) | async-done | bytes 1572880 | tf_op jit(solution)/shard_map/all_gather | solution.py:121
  (176 shorter events, 118.6 us)
Async XLA Ops:
  7.2 17.2 %copy-start = (bf16[1,1024,1024]{2,1,0:T(8,128)(2,1)S(1)}, bf16[1,1024,1024]{2,1,0:T(8,128)(2,1)}, u32[]{:S(2)}) copy-start(bf16[1,1024,1024]{2,1,0:T(8,128)(2,1)} %param.13) | copy-start | bytes 6291460
  7.2 191.0 %reduce-scatter.17.cloned.1.call-start = ((), (), s32[]{:S(2)}) async-start(), calls=%async_computation.7 | async-start | bytes 4718592 | tf_op jit(solution)/shard_map/reduce_scatter | solution.py:117
  20.2 4.2 copy-start.7
  33.9 4.1 collective-permute-start
  38.2 5.1 copy-start.2
  44.7 5.1 copy-start.8
  44.7 5.1 copy-start.11
  55.2 86.6 %copy-start.1 = (f32[256,1024]{1,0:T(8,128)}, f32[256,1024]{1,0:T(8,128)S(1)}, u32[]{:S(2)}) copy-start(f32[256,1024]{1,0:T(8,128)S(1)} %get-tuple-element.37) | copy-start | bytes 3145732
  85.2 5.5 copy-start.3
  85.3 5.5 copy-start.15
  85.3 5.5 copy-start.21
  92.2 4.1 collective-permute-start.1
  97.5 5.4 copy-start.16
  107.2 182.2 %reduce-scatter.21.cloned.1.call-start = ((), (), s32[]{:S(2)}) async-start(), calls=%async_computation.12 | async-start | bytes 4718592
  141.4 213.1 %reduce-scatter.25.cloned.1.call-start = ((), (), s32[]{:S(2)}) async-start(), calls=%async_computation.14 | async-start | bytes 589824
  141.8 4.2 copy-start.17
  172.0 246.9 %reduce-scatter.23.cloned.1.call-start = ((), (), s32[]{:S(2)}) async-start(), calls=%async_computation.13 | async-start | bytes 589824
  173.2 366.2 %reduce-scatter.15.cloned.1.call-start = ((), (), s32[]{:S(2)}) async-start(), calls=%async_computation.6 | async-start | bytes 7077888 | tf_op jit(solution)/shard_map/reduce_scatter | solution.py:117
  179.5 430.3 %reduce-scatter.19.cloned.1.call-start = ((), (), s32[]{:S(2)}) async-start(), calls=%async_computation.11 | async-start | bytes 2359296
  198.2 433.5 %all-gather.12.cloned.1.call-start = ((), (), s32[]{:S(2)}) async-start(), calls=%async_computation.9 | async-start | bytes 1572864 | tf_op jit(solution)/shard_map/all_gather | solution.py:121
  198.9 456.2 %all-gather.14.cloned.1.call-start = ((), (), s32[]{:S(2)}) async-start(), calls=%async_computation.10 | async-start | bytes 1572864 | tf_op jit(solution)/shard_map/all_gather | solution.py:121
  295.6 388.3 %all-gather.10.cloned.1.call-start = ((), (), s32[]{:S(2)}) async-start(), calls=%async_computation.8 | async-start | bytes 2359296 | tf_op jit(solution)/shard_map/all_gather | solution.py:121
  295.7 5.5 copy-start.4
  295.7 5.5 copy-start.18
  (13 other events, 17.4 us)
Sparse Core Ops, SparseCore 0:
  107.3 90.1 reduce-scatter.16
  201.5 87.8 reduce-scatter.20
  292.8 61.6 reduce-scatter.24
  358.0 60.8 reduce-scatter.22
  422.3 117.0 reduce-scatter.14
  542.8 66.9 reduce-scatter.18
  611.4 20.2 all-gather.11
  633.8 21.2 all-gather.13
  656.7 27.2 all-gather.9
